TPU v7x, 32 devices: a whole 2x2x4 slice. The times are simulated.
32 devices in a mesh: dp: 16 (over z, y, x), mp: 2 (over core).
Axes of the slice: x: 2, y: 2, z: 4, core: 2. Of those that a mesh axis runs over, the one named last changes fastest.
Arguments:
- store_rows: bfloat16 [8192, 4096], P('dp', 'mp'), may hold values from -64 to 64
- norm_gain: bfloat16 [4096], replicated, may hold values from 0.099609375 to 1.8984375
- key_weight: bfloat16 [4096, 2048], P(None, 'mp'), may hold values from -0.09375 to 0.09375
- value_weight: bfloat16 [4096, 2048], P(None, 'mp'), may hold values from -0.09375 to 0.09375
- queries: bfloat16 [128, 2048], P('dp', 'mp'), may hold values from -300 to 300
- counts: int32 [16], replicated, may hold values from 1 to 8, 32 in all
- slot_plan: int32 [32], P('dp'), may hold values from 0 to 31, each once
Outputs:
- context: bfloat16 [128, 2048], P('dp', 'mp')
All inputs are finite; a program needn't handle non-finite values.
Results may differ from a plain program's by a relative error of at most 0.0091.
Values may be sent and summed in bfloat16 or wider, within the bound.
A program may use at most 64 MiB of HBM per device.

v0:
```python
import jax
import jax.numpy as jnp
from jax import lax
from jax.sharding import PartitionSpec as P

HEAD_DIM = 64
norm_eps = 1e-06
score_scale = 0.125
far_below = -1e30


def local(store_rows, norm_gain, key_weight, value_weight, queries, counts, slot_plan):
    full_width = norm_gain.shape[0]
    row_count = store_rows.shape[0]
    local_cols = store_rows.shape[1]
    head_cols = key_weight.shape[1]
    heads_here = head_cols // HEAD_DIM
    passages_here = slot_plan.shape[0]
    seq_len = row_count // passages_here
    gain_full = norm_gain.astype(jnp.float32)
    raw_rows = store_rows.astype(jnp.float32)
    own_gain = lax.dynamic_slice_in_dim(gain_full, lax.axis_index("mp") * local_cols, local_cols, 0)
    scaled = (raw_rows * own_gain[None, :]).astype(jnp.bfloat16)
    total_sq = lax.psum(jnp.sum(raw_rows * raw_rows, axis=1), "mp")
    shard_part = lax.all_gather(scaled, "mp", axis=1, tiled=True)
    key_acc = jnp.dot(shard_part, key_weight, preferred_element_type=jnp.float32)
    value_acc = jnp.dot(shard_part, value_weight, preferred_element_type=jnp.float32)
    inv_rms = lax.rsqrt(total_sq / full_width + norm_eps)
    key_rows = (key_acc * inv_rms[:, None]).astype(jnp.bfloat16)
    value_rows = (value_acc * inv_rms[:, None]).astype(jnp.bfloat16)
    ends = jnp.cumsum(counts)
    slot_question = jnp.sum((slot_plan[:, None] >= ends[None, :]).astype(jnp.int32), axis=1)
    num_questions = counts.shape[0]
    dec_len = queries.shape[0]
    gathered = lax.all_gather(queries, "dp", axis=0, tiled=True)
    query_table = gathered.reshape(num_questions, dec_len, heads_here, HEAD_DIM)
    slot_queries = jnp.take(query_table, slot_question, axis=0)
    key_blocks = key_rows.reshape(passages_here, seq_len, heads_here, HEAD_DIM)
    value_blocks = value_rows.reshape(passages_here, seq_len, heads_here, HEAD_DIM).astype(
        jnp.float32
    )
    scores = (
        jnp.einsum("pihd,pthd->piht", slot_queries, key_blocks, preferred_element_type=jnp.float32)
        * score_scale
    )
    slot_max = jnp.max(scores, axis=3)
    member = slot_question[None, :] == jnp.arange(num_questions, dtype=jnp.int32)[:, None]
    member_float = member.astype(jnp.float32)
    question_max = jnp.max(jnp.where(member[:, :, None, None], slot_max[None], far_below), axis=1)
    max_level = lax.pmax(question_max, "dp")
    slot_level = jnp.take(max_level, slot_question, axis=0)
    weights = jnp.exp(scores - slot_level[..., None])
    slot_den = jnp.sum(weights, axis=3)
    slot_num = jnp.einsum("piht,pthd->pihd", weights, value_blocks, precision=lax.Precision.HIGHEST)
    slot_num = slot_num.reshape(passages_here, dec_len, head_cols)
    numerator = jnp.einsum("qp,pik->qik", member_float, slot_num, precision=lax.Precision.HIGHEST)
    denominator = jnp.einsum("qp,pih->qih", member_float, slot_den, precision=lax.Precision.HIGHEST)
    numerator, denominator = (numerator, denominator)
    summed_num, summed_den = (
        lax.psum_scatter(numerator, "dp", scatter_dimension=0, tiled=True),
        lax.psum_scatter(denominator, "dp", scatter_dimension=0, tiled=True),
    )
    own_num = summed_num[0]
    own_den = summed_den[0]
    context = own_num.reshape(dec_len, heads_here, HEAD_DIM) / own_den[..., None]
    return context.reshape(dec_len, head_cols).astype(jnp.bfloat16)


def solution(mesh):
    placed = (P("dp", "mp"), P(), P(None, "mp"), P(None, "mp"), P("dp", "mp"), P(), P("dp"))
    return jax.shard_map(
        local, mesh=mesh, in_specs=placed, out_specs=P("dp", "mp"), check_vma=False
    )
```

profile of v0, /device:TPU:0, one launch (start us, length us, event | category | flops | bytes accessed | tf_op | source)
XLA Modules:
  0.0 241.7 jit_solution(15678639214267508043)
XLA Ops:
  6.5 0.7 dynamic-slice_convert_fusion
  7.2 3.5 %fusion.1 = (f32[512]{0:T(512)S(1)}, bf16[512,2048]{1,0:T(8,128)(2,1)}) fusion(bf16[512,2048]{1,0:T(8,128)(2,1)} %param.7, f32[2048]{0:T(1024)S(1)} %dynamic-slice_convert_fusion), kind=kLoop, calls=%fused_computation.5 | loop fusion | flops 5242368 | bytes 4204544 | tf_op jit(solution)/shard_map/reduce_sum | solution.py:24
  10.8 0.6 copy-done.1
  11.7 0.2 fusion.23
  12.0 43.8 %all_gather.7 = bf16[128,1024]{1,0:T(8,128)(2,1)S(1)} all-gather(bf16[8,1024]{1,0:T(8,128)(2,1)S(1)} %copy-done), channel_id=1, replica_groups=mesh['dp'=16,'mp'=2] {'dp'}, dimensions={0}, use_global_device_ids=true | all-gather | bytes 278528 | tf_op jit(solution)/shard_map/all_gather | solution.py:35
  55.8 0.3 reshape.86
  56.2 0.6 gather_fusion
  56.7 2.5 %psum.7 = f32[512]{0:T(512)S(1)} all-reduce(f32[512]{0:T(512)S(1)} %get-tuple-element.5), channel_id=1, replica_groups=mesh['dp'=16,'mp'=2] {'mp'}, use_global_device_ids=true, to_apply=%region_3.4 | all-reduce | flops 512 | bytes 4096 | tf_op jit(solution)/shard_map/psum | solution.py:24
  59.3 9.1 %multiply_convert_fusion.1 = bf16[512,1024]{1,0:T(8,128)(2,1)S(1)} fusion(bf16[512,4096]{1,0:T(8,128)(2,1)} %all-gather.2.cloned.1.call-done, bf16[4096,1024]{1,0:T(8,128)(2,1)} %param.10, f32[512]{0:T(512)S(1)} %add_rsqrt_fusion), kind=kOutput, calls=%fused_computation.11 | convolution fusion | flops 4296015872 | bytes 13633536 | tf_op jit(solution)/shard_map/dot_general | solution.py:27
  68.4 1.3 reshape.105
  69.8 9.1 %multiply_convert_fusion = bf16[512,1024]{1,0:T(8,128)(2,1)S(1)} fusion(bf16[512,4096]{1,0:T(8,128)(2,1)} %all-gather.2.cloned.1.call-done, bf16[4096,1024]{1,0:T(8,128)(2,1)} %param.9, f32[512]{0:T(512)S(1)} %add_rsqrt_fusion), kind=kOutput, calls=%fused_computation.10 | convolution fusion | flops 4296015872 | bytes 13633536 | tf_op jit(solution)/shard_map/dot_general | solution.py:26
  78.9 2.4 reshape.106
  81.3 2.3 fusion.25
  83.8 72.0 %pmax.7 = f32[16,8,16]{2,1,0:T(8,128)S(1)} all-reduce(f32[16,8,16]{2,1,0:T(8,128)S(1)} %select_reduce_fusion), channel_id=1, replica_groups=mesh['dp'=16,'mp'=2] {'dp'}, use_global_device_ids=true, to_apply=%region_6.7 | all-reduce | flops 2048 | bytes 16384 | tf_op jit(solution)/shard_map/pmax | solution.py:50
  155.8 0.5 gather_fusion.1
  156.5 1.2 fusion.12
  157.9 0.5 fusion.21
  158.4 1.1 copy.47
  159.5 0.6 dynamic-slice
  160.1 0.2 fusion.15
  160.4 0.3 fusion.19
  160.7 71.9 %all-reduce = f32[16,8,16]{2,1,0:T(8,128)S(1)} all-reduce(f32[16,8,16]{2,1,0:T(8,128)S(1)} %copy.49), channel_id=3, replica_groups=mesh['dp'=16,'mp'=2] {'dp'}, use_global_device_ids=true, to_apply=%region_9.10.clone | all-reduce | flops 2048 | bytes 16384
  232.7 0.6 dynamic-slice_bitcast_fusion
  233.5 1.4 fusion.18
  (33 shorter events, 1.4 us)
Async XLA Ops:
  6.5 52.8 %all-gather.2.cloned.1.call-start = ((), (), s32[]{:S(2)}) async-start(), calls=%async_computation.1 | async-start | bytes 6291456 | tf_op jit(solution)/shard_map/all_gather | solution.py:25
  10.8 0.7 copy-start.1
  10.8 0.9 copy-start.2
  10.8 1.3 copy-start
  10.8 222.7 %reduce-scatter.2.cloned.1.call-start = ((), (), s32[]{:S(2)}) async-start(), calls=%async_computation.2 | async-start | bytes 557056 | tf_op jit(solution)/shard_map/reduce_scatter | solution.py:60
  157.7 1.8 copy-start.3
Sparse Core Ops, SparseCore 0:
  10.9 16.3 all-gather.1
  159.6 72.4 reduce-scatter.1
where the time goes:
time: 242 us
  blocking collectives  190 us (79%)
  matrix products  22.6 us (9%)
  between operations  13.6 us (6%)
  local copies, waits for them, and re-layouts  8.82 us (4%)
  other arithmetic  6.49 us (3%)
    pmax x1, blocking collectives, local(): max_level = lax.pmax(question_max, 'dp')  72 us
    unnamed x1, blocking collectives  71.9 us
    all_gather x1, blocking collectives, local(): gathered = lax.all_gather(queries, 'dp', axis=0, tiled=True)  43.8 us
    dot_general x1, matrix products, local(): jnp.dot(shard_part, key_weight, preferred_element_type=jnp.float32)  9.15 us
    dot_general x1, matrix products, local(): jnp.dot(shard_part, value_weight, preferred_element_type=jnp.float32)  9.15 us
  transfers between devices with their start and end apart: 2, of which 0 were waited for; matrix products, arithmetic and copies ran while one was open for 1% of the time, Pallas kernels for 0%

commit v1 on v0

--- a/solution.py
+++ b/solution.py
@@ -32,7 +32,22 @@
     slot_question = jnp.sum((slot_plan[:, None] >= ends[None, :]).astype(jnp.int32), axis=1)
     num_questions = counts.shape[0]
     dec_len = queries.shape[0]
-    gathered = lax.all_gather(queries, "dp", axis=0, tiled=True)
+    ways, here, step = (lax.axis_size("dp"), lax.axis_index("dp"), queries.shape[0])
+    shape = [n * ways if d == 0 else n for d, n in enumerate(queries.shape)]
+    gathered = lax.dynamic_update_slice_in_dim(
+        jnp.zeros(shape, queries.dtype), queries, here * step, axis=0
+    )
+    going_up = going_down = queries
+    for far in range(1, ways // 2 + 1):
+        going_up = lax.ppermute(going_up, "dp", [(d, (d + 1) % ways) for d in range(ways)])
+        gathered = lax.dynamic_update_slice_in_dim(
+            gathered, going_up, (here - far) % ways * step, axis=0
+        )
+        if 2 * far < ways:
+            going_down = lax.ppermute(going_down, "dp", [(d, (d - 1) % ways) for d in range(ways)])
+            gathered = lax.dynamic_update_slice_in_dim(
+                gathered, going_down, (here + far) % ways * step, axis=0
+            )
     query_table = gathered.reshape(num_questions, dec_len, heads_here, HEAD_DIM)
     slot_queries = jnp.take(query_table, slot_question, axis=0)
     key_blocks = key_rows.reshape(passages_here, seq_len, heads_here, HEAD_DIM)

time: 242 us -> 263 us (1.087)
  blocking collectives: 190 us -> 146 us
  starting transfers between devices: 0.04 us -> 42.1 us
  waiting for transfers between devices: 0.05 us -> 21.8 us
    all_gather x1 -> x0, blocking collectives: 43.8 us -> none  [local(): gathered = lax.all_gather(queries, 'dp', axis=0, tiled=True)]
    ppermute x0 -> x15, starting transfers between devices: none -> 42.1 us  [the longest x7 42.1 us: local(): lax.ppermute(going_down, 'dp', [(d, (d - 1) % ways) for d in range(ways)])]
    ppermute x0 -> x15, waiting for transfers between devices: none -> 21.7 us  [the longest x8 14.6 us: local(): lax.ppermute(going_up, 'dp', [(d, (d + 1) % ways) for d in range(ways)])]
  transfers between devices with their start and end apart: 2 -> 17, of which waited for: 0 -> 7; matrix products, arithmetic and copies ran while one was open for 1% -> 1% of each run, Pallas kernels for 0% -> 0%
where the time goes in v1:
time: 263 us; the launch traced here: 262 us
  blocking collectives  146 us (56%)
  starting transfers between devices  42.1 us (16%)
  matrix products  22.6 us (9%)
  waiting for transfers between devices  21.8 us (8%)
  between operations  13.9 us (5%)
  local copies, waits for them, and re-layouts  9 us (3%)
  other arithmetic  6.48 us (2%)
    pmax x1, blocking collectives, local(): max_level = lax.pmax(question_max, 'dp')  72 us
    unnamed x1, blocking collectives  71.9 us
    ppermute x7, starting transfers between devices, local(): lax.ppermute(going_down, 'dp', [(d, (d - 1) % ways) for d in range(ways)])  42.1 us
    ppermute x8, waiting for transfers between devices, local(): lax.ppermute(going_up, 'dp', [(d, (d + 1) % ways) for d in range(ways)])  14.6 us
    dot_general x1, matrix products, local(): jnp.dot(shard_part, key_weight, preferred_element_type=jnp.float32)  9.15 us
    dot_general x1, matrix products, local(): jnp.dot(shard_part, value_weight, preferred_element_type=jnp.float32)  9.15 us
    ppermute x7, waiting for transfers between devices, local(): lax.ppermute(going_down, 'dp', [(d, (d - 1) % ways) for d in range(ways)])  7.08 us
  transfers between devices with their start and end apart: 17, of which 7 were waited for; matrix products, arithmetic and copies ran while one was open for 1% of the time, Pallas kernels for 0%

profile of v1, /device:TPU:0, one launch (start us, length us, event | category | flops | bytes accessed | tf_op | source)
XLA Modules:
  0.0 262.3 jit_solution(3879171532434962550)
XLA Ops:
  7.2 3.5 %fusion.1 = (f32[512]{0:T(512)S(1)}, bf16[512,2048]{1,0:T(8,128)(2,1)}) fusion(bf16[512,2048]{1,0:T(8,128)(2,1)} %param.7, f32[2048]{0:T(1024)S(1)} %dynamic-slice_convert_fusion), kind=kLoop, calls=%fused_computation.5 | loop fusion | flops 5242368 | bytes 4204544 | tf_op jit(solution)/shard_map/reduce_sum | solution.py:24
  11.5 6.9 %collective-permute-start.1 = (bf16[8,1024]{1,0:T(8,128)(2,1)S(1)}, bf16[8,1024]{1,0:T(8,128)(2,1)S(1)}, u32[]{:S(2)}, u32[]{:S(2)}) collective-permute-start(bf16[8,1024]{1,0:T(8,128)(2,1)S(1)} %copy-done), channel_id=1, source_target_pairs={{0,30},{2,0},{4,2},{6,4},{8,6},{10,8},{12,10},{14,12},{16,14},{18,... | collective-permute-start | bytes 49160 | tf_op jit(solution)/shard_map/ppermute | solution.py:47
  18.6 2.5 psum.7
  21.8 5.7 %collective-permute-start.3 = (bf16[8,1024]{1,0:T(8,128)(2,1)S(1)}, bf16[8,1024]{1,0:T(8,128)(2,1)S(1)}, u32[]{:S(2)}, u32[]{:S(2)}) collective-permute-start(bf16[8,1024]{1,0:T(8,128)(2,1)S(1)} %collective-permute-done.1), channel_id=1, source_target_pairs={{0,30},{2,0},{4,2},{6,4},{8,6},{10,8},{12,10},{14,12},{16,14},{18,... | collective-permute-start | bytes 49160 | tf_op jit(solution)/shard_map/ppermute | solution.py:47
  27.5 1.4 collective-permute-done.3
  28.9 5.9 %collective-permute-start.5 = (bf16[8,1024]{1,0:T(8,128)(2,1)S(1)}, bf16[8,1024]{1,0:T(8,128)(2,1)S(1)}, u32[]{:S(2)}, u32[]{:S(2)}) collective-permute-start(bf16[8,1024]{1,0:T(8,128)(2,1)S(1)} %collective-permute-done.3), channel_id=1, source_target_pairs={{0,30},{2,0},{4,2},{6,4},{8,6},{10,8},{12,10},{14,12},{16,14},{18,... | collective-permute-start | bytes 49160 | tf_op jit(solution)/shard_map/ppermute | solution.py:47
  34.9 1.4 collective-permute-done.5
  36.3 5.9 %collective-permute-start.7 = (bf16[8,1024]{1,0:T(8,128)(2,1)S(1)}, bf16[8,1024]{1,0:T(8,128)(2,1)S(1)}, u32[]{:S(2)}, u32[]{:S(2)}) collective-permute-start(bf16[8,1024]{1,0:T(8,128)(2,1)S(1)} %collective-permute-done.5), channel_id=1, source_target_pairs={{0,30},{2,0},{4,2},{6,4},{8,6},{10,8},{12,10},{14,12},{16,14},{18,... | collective-permute-start | bytes 49160 | tf_op jit(solution)/shard_map/ppermute | solution.py:47
  42.2 1.4 collective-permute-done.7
  43.6 5.9 %collective-permute-start.9 = (bf16[8,1024]{1,0:T(8,128)(2,1)S(1)}, bf16[8,1024]{1,0:T(8,128)(2,1)S(1)}, u32[]{:S(2)}, u32[]{:S(2)}) collective-permute-start(bf16[8,1024]{1,0:T(8,128)(2,1)S(1)} %collective-permute-done.7), channel_id=1, source_target_pairs={{0,30},{2,0},{4,2},{6,4},{8,6},{10,8},{12,10},{14,12},{16,14},{18,... | collective-permute-start | bytes 49160 | tf_op jit(solution)/shard_map/ppermute | solution.py:47
  49.5 1.4 collective-permute-done.9
  50.9 5.9 %collective-permute-start.11 = (bf16[8,1024]{1,0:T(8,128)(2,1)S(1)}, bf16[8,1024]{1,0:T(8,128)(2,1)S(1)}, u32[]{:S(2)}, u32[]{:S(2)}) collective-permute-start(bf16[8,1024]{1,0:T(8,128)(2,1)S(1)} %collective-permute-done.9), channel_id=1, source_target_pairs={{0,30},{2,0},{4,2},{6,4},{8,6},{10,8},{12,10},{14,12},{16,14},{18,... | collective-permute-start | bytes 49160 | tf_op jit(solution)/shard_map/ppermute | solution.py:47
  56.9 1.4 collective-permute-done.11
  58.3 5.9 %collective-permute-start.13 = (bf16[8,1024]{1,0:T(8,128)(2,1)S(1)}, bf16[8,1024]{1,0:T(8,128)(2,1)S(1)}, u32[]{:S(2)}, u32[]{:S(2)}) collective-permute-start(bf16[8,1024]{1,0:T(8,128)(2,1)S(1)} %collective-permute-done.11), channel_id=1, source_target_pairs={{0,30},{2,0},{4,2},{6,4},{8,6},{10,8},{12,10},{14,12},{16,14},{18,... | collective-permute-start | bytes 49160 | tf_op jit(solution)/shard_map/ppermute | solution.py:47
  64.2 7.3 %collective-permute-done.12 = bf16[8,1024]{1,0:T(8,128)(2,1)S(1)} collective-permute-done((bf16[8,1024]{1,0:T(8,128)(2,1)S(1)}, bf16[8,1024]{1,0:T(8,128)(2,1)S(1)}, u32[]{:S(2)}, u32[]{:S(2)}) %collective-permute-start.12) | collective-permute-done | bytes 16416 | tf_op jit(solution)/shard_map/ppermute | solution.py:42
  71.5 7.3 %collective-permute-done.14 = bf16[8,1024]{1,0:T(8,128)(2,1)S(1)} collective-permute-done((bf16[8,1024]{1,0:T(8,128)(2,1)S(1)}, bf16[8,1024]{1,0:T(8,128)(2,1)S(1)}, u32[]{:S(2)}, u32[]{:S(2)}) %collective-permute-start.14) | collective-permute-done | bytes 16416 | tf_op jit(solution)/shard_map/ppermute | solution.py:42
  79.8 9.1 %multiply_convert_fusion.1 = bf16[512,1024]{1,0:T(8,128)(2,1)S(1)} fusion(bf16[512,4096]{1,0:T(8,128)(2,1)} %all-gather.2.cloned.1.call-done, bf16[4096,1024]{1,0:T(8,128)(2,1)} %param.10, f32[512]{0:T(512)S(1)} %add_rsqrt_fusion), kind=kOutput, calls=%fused_computation.11 | convolution fusion | flops 4296015872 | bytes 13633536 | tf_op jit(solution)/shard_map/dot_general | solution.py:27
  89.0 1.3 reshape.105
  90.3 9.1 %multiply_convert_fusion = bf16[512,1024]{1,0:T(8,128)(2,1)S(1)} fusion(bf16[512,4096]{1,0:T(8,128)(2,1)} %all-gather.2.cloned.1.call-done, bf16[4096,1024]{1,0:T(8,128)(2,1)} %param.9, f32[512]{0:T(512)S(1)} %add_rsqrt_fusion), kind=kOutput, calls=%fused_computation.10 | convolution fusion | flops 4296015872 | bytes 13633536 | tf_op jit(solution)/shard_map/dot_general | solution.py:26
  99.5 2.4 reshape.106
  101.9 2.3 fusion.25
  104.4 72.0 %pmax.7 = f32[16,8,16]{2,1,0:T(8,128)S(1)} all-reduce(f32[16,8,16]{2,1,0:T(8,128)S(1)} %select_reduce_fusion), channel_id=1, replica_groups=mesh['dp'=16,'mp'=2] {'dp'}, use_global_device_ids=true, to_apply=%region_6.7 | all-reduce | flops 2048 | bytes 16384 | tf_op jit(solution)/shard_map/pmax | solution.py:65
  181.3 71.9 %all-reduce = f32[16,8,16]{2,1,0:T(8,128)S(1)} all-reduce(f32[16,8,16]{2,1,0:T(8,128)S(1)} %copy.49), channel_id=3, replica_groups=mesh['dp'=16,'mp'=2] {'dp'}, use_global_device_ids=true, to_apply=%region_9.10.clone | all-reduce | flops 2048 | bytes 16384
  254.1 1.4 fusion.18
  (79 shorter events, 9.0 us)
Async XLA Ops:
  6.5 73.3 %all-gather.2.cloned.1.call-start = ((), (), s32[]{:S(2)}) async-start(), calls=%async_computation.1 | async-start | bytes 6291456 | tf_op jit(solution)/shard_map/all_gather | solution.py:25
  10.7 0.7 copy-start
  10.8 7.7 %copy-start.1 = (s32[16]{0:T(128)S(1)}, s32[16]{0:T(128)}, u32[]{:S(2)}) copy-start(s32[16]{0:T(128)} %param.12) | copy-start | bytes 196
  10.8 10.4 %copy-start.2 = (s32[2]{0:T(128)S(1)}, s32[2]{0:T(128)}, u32[]{:S(2)}) copy-start(s32[2]{0:T(128)} %param.13) | copy-start | bytes 28
  10.8 243.3 %reduce-scatter.2.cloned.1.call-start = ((), (), s32[]{:S(2)}) async-start(), calls=%async_computation.2 | async-start | bytes 557056 | tf_op jit(solution)/shard_map/reduce_scatter | solution.py:75
  11.5 10.3 %collective-permute-start.1 = (bf16[8,1024]{1,0:T(8,128)(2,1)S(1)}, bf16[8,1024]{1,0:T(8,128)(2,1)S(1)}, u32[]{:S(2)}, u32[]{:S(2)}) collective-permute-start(bf16[8,1024]{1,0:T(8,128)(2,1)S(1)} %copy-done), channel_id=1, source_target_pairs={{0,30},{2,0},{4,2},{6,4},{8,6},{10,8},{12,10},{14,12},{16,14},{18,... | collective-permute-start | bytes 49160 | tf_op jit(solution)/shard_map/ppermute | solution.py:47
  18.4 9.1 %collective-permute-start = (bf16[8,1024]{1,0:T(8,128)(2,1)S(1)}, bf16[8,1024]{1,0:T(8,128)(2,1)S(1)}, u32[]{:S(2)}, u32[]{:S(2)}) collective-permute-start(bf16[8,1024]{1,0:T(8,128)(2,1)S(1)} %copy-done), channel_id=1, source_target_pairs={{0,2},{2,4},{4,6},{6,8},{8,10},{10,12},{12,14},{14,16},{16,18},{18... | collective-permute-start | bytes 49160 | tf_op jit(solution)/shard_map/ppermute | solution.py:42
  21.8 7.1 %collective-permute-start.3 = (bf16[8,1024]{1,0:T(8,128)(2,1)S(1)}, bf16[8,1024]{1,0:T(8,128)(2,1)S(1)}, u32[]{:S(2)}, u32[]{:S(2)}) collective-permute-start(bf16[8,1024]{1,0:T(8,128)(2,1)S(1)} %collective-permute-done.1), channel_id=1, source_target_pairs={{0,30},{2,0},{4,2},{6,4},{8,6},{10,8},{12,10},{14,12},{16,14},{18,... | collective-permute-start | bytes 49160 | tf_op jit(solution)/shard_map/ppermute | solution.py:47
  27.5 7.3 %collective-permute-start.2 = (bf16[8,1024]{1,0:T(8,128)(2,1)S(1)}, bf16[8,1024]{1,0:T(8,128)(2,1)S(1)}, u32[]{:S(2)}, u32[]{:S(2)}) collective-permute-start(bf16[8,1024]{1,0:T(8,128)(2,1)S(1)} %collective-permute-done), channel_id=1, source_target_pairs={{0,2},{2,4},{4,6},{6,8},{8,10},{10,12},{12,14},{14,16},{16,18},{18... | collective-permute-start | bytes 49160 | tf_op jit(solution)/shard_map/ppermute | solution.py:42
  28.9 7.3 %collective-permute-start.5 = (bf16[8,1024]{1,0:T(8,128)(2,1)S(1)}, bf16[8,1024]{1,0:T(8,128)(2,1)S(1)}, u32[]{:S(2)}, u32[]{:S(2)}) collective-permute-start(bf16[8,1024]{1,0:T(8,128)(2,1)S(1)} %collective-permute-done.3), channel_id=1, source_target_pairs={{0,30},{2,0},{4,2},{6,4},{8,6},{10,8},{12,10},{14,12},{16,14},{18,... | collective-permute-start | bytes 49160 | tf_op jit(solution)/shard_map/ppermute | solution.py:47
  34.8 7.3 %collective-permute-start.4 = (bf16[8,1024]{1,0:T(8,128)(2,1)S(1)}, bf16[8,1024]{1,0:T(8,128)(2,1)S(1)}, u32[]{:S(2)}, u32[]{:S(2)}) collective-permute-start(bf16[8,1024]{1,0:T(8,128)(2,1)S(1)} %collective-permute-done.2), channel_id=1, source_target_pairs={{0,2},{2,4},{4,6},{6,8},{8,10},{10,12},{12,14},{14,16},{16,18},{18... | collective-permute-start | bytes 49160 | tf_op jit(solution)/shard_map/ppermute | solution.py:42
  36.3 7.3 %collective-permute-start.7 = (bf16[8,1024]{1,0:T(8,128)(2,1)S(1)}, bf16[8,1024]{1,0:T(8,128)(2,1)S(1)}, u32[]{:S(2)}, u32[]{:S(2)}) collective-permute-start(bf16[8,1024]{1,0:T(8,128)(2,1)S(1)} %collective-permute-done.5), channel_id=1, source_target_pairs={{0,30},{2,0},{4,2},{6,4},{8,6},{10,8},{12,10},{14,12},{16,14},{18,... | collective-permute-start | bytes 49160 | tf_op jit(solution)/shard_map/ppermute | solution.py:47
  42.2 7.3 %collective-permute-start.6 = (bf16[8,1024]{1,0:T(8,128)(2,1)S(1)}, bf16[8,1024]{1,0:T(8,128)(2,1)S(1)}, u32[]{:S(2)}, u32[]{:S(2)}) collective-permute-start(bf16[8,1024]{1,0:T(8,128)(2,1)S(1)} %collective-permute-done.4), channel_id=1, source_target_pairs={{0,2},{2,4},{4,6},{6,8},{8,10},{10,12},{12,14},{14,16},{16,18},{18... | collective-permute-start | bytes 49160 | tf_op jit(solution)/shard_map/ppermute | solution.py:42
  43.6 7.3 %collective-permute-start.9 = (bf16[8,1024]{1,0:T(8,128)(2,1)S(1)}, bf16[8,1024]{1,0:T(8,128)(2,1)S(1)}, u32[]{:S(2)}, u32[]{:S(2)}) collective-permute-start(bf16[8,1024]{1,0:T(8,128)(2,1)S(1)} %collective-permute-done.7), channel_id=1, source_target_pairs={{0,30},{2,0},{4,2},{6,4},{8,6},{10,8},{12,10},{14,12},{16,14},{18,... | collective-permute-start | bytes 49160 | tf_op jit(solution)/shard_map/ppermute | solution.py:47
  49.5 7.3 %collective-permute-start.8 = (bf16[8,1024]{1,0:T(8,128)(2,1)S(1)}, bf16[8,1024]{1,0:T(8,128)(2,1)S(1)}, u32[]{:S(2)}, u32[]{:S(2)}) collective-permute-start(bf16[8,1024]{1,0:T(8,128)(2,1)S(1)} %collective-permute-done.6), channel_id=1, source_target_pairs={{0,2},{2,4},{4,6},{6,8},{8,10},{10,12},{12,14},{14,16},{16,18},{18... | collective-permute-start | bytes 49160 | tf_op jit(solution)/shard_map/ppermute | solution.py:42
  50.9 7.3 %collective-permute-start.11 = (bf16[8,1024]{1,0:T(8,128)(2,1)S(1)}, bf16[8,1024]{1,0:T(8,128)(2,1)S(1)}, u32[]{:S(2)}, u32[]{:S(2)}) collective-permute-start(bf16[8,1024]{1,0:T(8,128)(2,1)S(1)} %collective-permute-done.9), channel_id=1, source_target_pairs={{0,30},{2,0},{4,2},{6,4},{8,6},{10,8},{12,10},{14,12},{16,14},{18,... | collective-permute-start | bytes 49160 | tf_op jit(solution)/shard_map/ppermute | solution.py:47
  56.8 7.3 %collective-permute-start.10 = (bf16[8,1024]{1,0:T(8,128)(2,1)S(1)}, bf16[8,1024]{1,0:T(8,128)(2,1)S(1)}, u32[]{:S(2)}, u32[]{:S(2)}) collective-permute-start(bf16[8,1024]{1,0:T(8,128)(2,1)S(1)} %collective-permute-done.8), channel_id=1, source_target_pairs={{0,2},{2,4},{4,6},{6,8},{8,10},{10,12},{12,14},{14,16},{16,18},{18... | collective-permute-start | bytes 49160 | tf_op jit(solution)/shard_map/ppermute | solution.py:42
  58.3 13.2 %collective-permute-start.13 = (bf16[8,1024]{1,0:T(8,128)(2,1)S(1)}, bf16[8,1024]{1,0:T(8,128)(2,1)S(1)}, u32[]{:S(2)}, u32[]{:S(2)}) collective-permute-start(bf16[8,1024]{1,0:T(8,128)(2,1)S(1)} %collective-permute-done.11), channel_id=1, source_target_pairs={{0,30},{2,0},{4,2},{6,4},{8,6},{10,8},{12,10},{14,12},{16,14},{18,... | collective-permute-start | bytes 49160 | tf_op jit(solution)/shard_map/ppermute | solution.py:47
  64.2 7.3 %collective-permute-start.12 = (bf16[8,1024]{1,0:T(8,128)(2,1)S(1)}, bf16[8,1024]{1,0:T(8,128)(2,1)S(1)}, u32[]{:S(2)}, u32[]{:S(2)}) collective-permute-start(bf16[8,1024]{1,0:T(8,128)(2,1)S(1)} %collective-permute-done.10), channel_id=1, source_target_pairs={{0,2},{2,4},{4,6},{6,8},{8,10},{10,12},{12,14},{14,16},{16,18},{18... | collective-permute-start | bytes 49160 | tf_op jit(solution)/shard_map/ppermute | solution.py:42
  71.5 7.3 %collective-permute-start.14 = (bf16[8,1024]{1,0:T(8,128)(2,1)S(1)}, bf16[8,1024]{1,0:T(8,128)(2,1)S(1)}, u32[]{:S(2)}, u32[]{:S(2)}) collective-permute-start(bf16[8,1024]{1,0:T(8,128)(2,1)S(1)} %collective-permute-done.12), channel_id=1, source_target_pairs={{0,2},{2,4},{4,6},{6,8},{8,10},{10,12},{12,14},{14,16},{16,18},{18... | collective-permute-start | bytes 49160 | tf_op jit(solution)/shard_map/ppermute | solution.py:42
  178.3 1.8 copy-start.3
Sparse Core Ops, SparseCore 0:
  10.9 16.3 all-gather.1
  180.2 72.4 reduce-scatter.1
